TPU v7x, 32 devices: a whole 2x2x4 slice. The times are simulated.
32 devices in a mesh: gx: 4 (over y, core), gy: 8 (over z, x).
Axes of the slice: x: 2, y: 2, z: 4, core: 2. Of those that a mesh axis runs over, the one named last changes fastest.
Arguments:
- source: float32 [256, 128, 128], P('gx', 'gy'), may hold values from -6 to 6
- diagonal: float32 [256, 128, 128], P('gx', 'gy'), may hold values from 6.05 to 7
- face_x: float32 [256, 128, 128], P('gx', 'gy'), may hold values from 0.1 to 1
- face_y: float32 [256, 128, 128], P('gx', 'gy'), may hold values from 0.1 to 1
- face_z: float32 [256, 128, 128], P('gx', 'gy'), may hold values from 0.1 to 1
- iterates: float32 [8, 256, 128, 128], P(None, 'gx', 'gy'), may hold values from -0.3 to 0.3
- labels: int32 [256, 128], P('gx', 'gy'), may hold values from 0 to 7
Outputs:
- new_iterates: float32 [8, 256, 128, 128], P(None, 'gx', 'gy')
- new_residual: float32 [256, 128, 128], P('gx', 'gy')
All inputs are finite; a program needn't handle non-finite values.
Results may differ from a plain program's by a relative error of at most 0.0003.
Values sent between devices are 32-bit elements; how exact they have to be, the bound alone decides.
No kernel may reach another device: no remote copies, remote signals or barrier semaphores. Data moves between devices by JAX's collectives and lax.ppermute only.
A program may use at most 128 MiB of HBM per device.

v0:
```python
import jax
import jax.numpy as jnp
from jax import lax
from jax.sharding import PartitionSpec as P

ENLARGE = 8
basis_shift = 6.5


def padded_2(block, sides, width):
    for axis, dim in sides:
        count = lax.axis_size(axis)
        forward = [(i, i + 1) for i in range(count - 1)]
        backward = [(target, source) for source, target in forward]
        low = lax.ppermute(
            lax.slice_in_dim(block, block.shape[dim] - width, None, axis=dim), axis, forward
        )
        high = lax.ppermute(lax.slice_in_dim(block, 0, width, axis=dim), axis, backward)
        block = jnp.concatenate([low, block, high], axis=dim)
    return block


def stencil(values, face_x, face_y, face_z, diagonal):
    centre = values[..., 1:-1, 1:-1, :]
    result = diagonal * centre
    result = (
        result
        - face_x[1:-1, 1:-1, :] * values[..., 2:, 1:-1, :]
        - face_x[:-2, 1:-1, :] * values[..., :-2, 1:-1, :]
    )
    result = (
        result
        - face_y[1:-1, 1:-1, :] * values[..., 1:-1, 2:, :]
        - face_y[1:-1, :-2, :] * values[..., 1:-1, :-2, :]
    )
    widths = [(0, 0)] * (centre.ndim - 1) + [(1, 1)]
    padded = jnp.pad(centre, widths)
    lower_face = jnp.pad(face_z[..., :-1], ((0, 0), (0, 0), (1, 0)))
    return result - face_z * padded[..., 2:] - lower_face * padded[..., :-2]


def finish(gram, project):
    highest = lax.Precision.HIGHEST
    lower = jnp.linalg.cholesky(gram)
    ident = jnp.eye(gram.shape[0], dtype=gram.dtype)
    inverse = lax.linalg.triangular_solve(lower, ident, left_side=True, lower=True)
    reduced = jnp.dot(jnp.dot(inverse, project, precision=highest), inverse.T, precision=highest)
    reduced = 0.5 * (reduced + reduced.T)
    target = jnp.dot(inverse, gram[:, :ENLARGE], precision=highest)
    factor = jnp.linalg.cholesky(reduced)
    middle = lax.linalg.triangular_solve(factor, target, left_side=True, lower=True)
    solved = lax.linalg.triangular_solve(
        factor, middle, left_side=True, lower=True, transpose_a=True
    )
    return jnp.dot(inverse.T, solved, precision=highest)


def shards(source, diagonal, face_x, face_y, face_z, iterates, labels):
    highest = lax.Precision.HIGHEST
    summed = jnp.sum(iterates, axis=0)
    columns = jnp.arange(ENLARGE, dtype=jnp.int32)
    near = (
        padded_2(summed, (("gx", 0), ("gy", 1)), 1),
        padded_2(face_x, (("gx", 0), ("gy", 1)), 1),
        padded_2(face_y, (("gx", 0), ("gy", 1)), 1),
    )
    near_sum, near_fx, near_fy = near
    residual = source - stencil(near_sum, near_fx, near_fy, face_z, diagonal)
    onehot = (labels[None] == columns[:, None, None]).astype(jnp.float32)
    blocks = residual[None] * onehot[..., None]
    blocks_wide = padded_2(blocks, (("gx", 1), ("gy", 2)), 1)
    applied = stencil(blocks_wide, near_fx, near_fy, face_z, diagonal)
    powered = applied - basis_shift * blocks
    powered_wide = padded_2(powered, (("gx", 1), ("gy", 2)), 1)
    second = stencil(powered_wide, near_fx, near_fy, face_z, diagonal)
    basis = jnp.concatenate([blocks, powered], axis=0)
    image = jnp.concatenate([applied, second], axis=0)
    gram_local = jnp.einsum("aijk,bijk->ab", basis, basis, precision=highest)
    project_local = jnp.einsum("aijk,bijk->ab", basis, image, precision=highest)
    gram = lax.psum(gram_local, ("gx", "gy"))
    project = lax.psum(project_local, ("gx", "gy"))
    coeffs = finish(gram, project)
    new_iterates = iterates + jnp.einsum("ab,aijk->bijk", coeffs, basis, precision=highest)
    carried = jnp.sum(coeffs, axis=1)
    new_residual = residual - jnp.einsum("a,aijk->ijk", carried, image, precision=highest)
    return (new_iterates, new_residual)


def solution(mesh):
    placed = (
        P("gx", "gy", None),
        P("gx", "gy", None),
        P("gx", "gy", None),
        P("gx", "gy", None),
        P("gx", "gy", None),
        P(None, "gx", "gy", None),
        P("gx", "gy"),
    )
    return jax.shard_map(
        shards,
        mesh=mesh,
        in_specs=placed,
        out_specs=(P(None, "gx", "gy", None), P("gx", "gy", None)),
        check_vma=False,
    )
```

profile of v0, /device:TPU:0, one launch (start us, length us, event | category | flops | bytes accessed | tf_op | source)
XLA Modules:
  0.0 177.3 jit_solution(15040397435094770270)
XLA Ops:
  0.7 2.7 %reduce_sum.18 = f32[64,16,128]{2,1,0:T(8,128)S(1)} reduce(f32[8,64,16,128]{3,2,1,0:T(8,128)} %param.13, f32[]{:T(128)} %constant.43.clone.1), dimensions={0}, to_apply=%region_0.0 | reduce | flops 917504 | bytes 4718596 | tf_op jit(solution)/shard_map/reduce_sum | solution.py:60
  3.4 1.3 collective-permute-start
  4.7 3.0 %collective-permute-start.2 = (f32[1,16,128]{2,1,0:T(8,128)S(1)}, f32[1,16,128]{2,1,0:T(8,128)S(1)}, u32[]{:S(2)}, u32[]{:S(2)}) collective-permute-start(f32[1,16,128]{2,1,0:T(8,128)S(1)} %get-tuple-element.23), channel_id=1, source_target_pairs={{0,8},{8,16},{16,24},{1,9},{9,17},{17,25},{2,10},{10,18},{18,26},{... | collective-permute-start | bytes 24584 | tf_op jit(solution)/shard_map/ppermute | solution.py:15
  7.7 4.5 %collective-permute-start.4 = (f32[1,16,128]{2,1,0:T(8,128)S(1)}, f32[1,16,128]{2,1,0:T(8,128)S(1)}, u32[]{:S(2)}, u32[]{:S(2)}) collective-permute-start(f32[1,16,128]{2,1,0:T(8,128)S(1)} %get-tuple-element.22), channel_id=1, source_target_pairs={{0,8},{8,16},{16,24},{1,9},{9,17},{17,25},{2,10},{10,18},{18,26},{... | collective-permute-start | bytes 24584 | tf_op jit(solution)/shard_map/ppermute | solution.py:15
  12.2 1.3 collective-permute-start.5
  13.6 3.0 %collective-permute-start.1 = (f32[1,16,128]{2,1,0:T(8,128)S(1)}, f32[1,16,128]{2,1,0:T(8,128)S(1)}, u32[]{:S(2)}, u32[]{:S(2)}) collective-permute-start(f32[1,16,128]{2,1,0:T(8,128)S(1)} %slice.156), channel_id=1, source_target_pairs={{0,8},{8,16},{16,24},{1,9},{9,17},{17,25},{2,10},{10,18},{18,26},{... | collective-permute-start | bytes 24584 | tf_op jit(solution)/shard_map/ppermute | solution.py:15
  16.8 1.3 collective-permute-start.3
  18.1 4.5 %collective-permute-start.7 = (f32[66,1,128]{2,1,0:T(1,128)S(1)}, f32[66,1,128]{2,1,0:T(1,128)S(1)}, u32[]{:S(2)}, u32[]{:S(2)}) collective-permute-start(f32[66,1,128]{2,1,0:T(1,128)S(1)} %get-tuple-element.20), channel_id=1, source_target_pairs={{0,1},{1,2},{2,3},{3,4},{4,5},{5,6},{6,7},{8,9},{9,10},{10,11},{11... | collective-permute-start | bytes 101384 | tf_op jit(solution)/shard_map/ppermute | solution.py:15
  22.7 4.3 %collective-permute-start.6 = (f32[66,1,128]{2,1,0:T(1,128)S(1)}, f32[66,1,128]{2,1,0:T(1,128)S(1)}, u32[]{:S(2)}, u32[]{:S(2)}) collective-permute-start(f32[66,1,128]{2,1,0:T(1,128)S(1)} %slice.194), channel_id=1, source_target_pairs={{0,1},{1,2},{2,3},{3,4},{4,5},{5,6},{6,7},{8,9},{9,10},{10,11},{11... | collective-permute-start | bytes 101384 | tf_op jit(solution)/shard_map/ppermute | solution.py:15
  27.1 0.2 fusion.43
  27.3 1.3 collective-permute-done.6
  28.6 1.6 fusion.33
  30.2 1.3 broadcast_multiply_fusion
  31.5 1.3 collective-permute-start.8
  32.8 3.0 %collective-permute-start.9 = (f32[8,1,16,128]{3,0,2,1:T(8,128)S(1)}, f32[8,1,16,128]{3,0,2,1:T(8,128)S(1)}, u32[]{:S(2)}, u32[]{:S(2)}) collective-permute-start(f32[8,1,16,128]{3,0,2,1:T(8,128)S(1)} %get-tuple-element.17), channel_id=1, source_target_pairs={{0,8},{8,16},{16,24},{1,9},{9,17},{17,25},{2,10},{10,18},{18,26},{... | collective-permute-start | bytes 196616 | tf_op jit(solution)/shard_map/ppermute | solution.py:15
  35.9 0.9 collective-permute-done.9
  36.8 1.3 collective-permute-start.10
  38.1 5.0 %collective-permute-start.11 = (f32[8,66,1,128]{3,0,2,1:T(8,128)S(1)}, f32[8,66,1,128]{3,0,2,1:T(8,128)S(1)}, u32[]{:S(2)}, u32[]{:S(2)}) collective-permute-start(f32[8,66,1,128]{3,0,2,1:T(8,128)S(1)} %get-tuple-element.14), channel_id=1, source_target_pairs={{0,1},{1,2},{2,3},{3,4},{4,5},{5,6},{6,7},{8,9},{9,10},{10,11},{11... | collective-permute-start | bytes 811016 | tf_op jit(solution)/shard_map/ppermute | solution.py:15
  43.1 0.2 pad.18
  43.4 4.0 %collective-permute-done.10 = f32[8,66,1,128]{3,0,2,1:T(8,128)S(1)} collective-permute-done((f32[8,66,1,128]{3,0,2,1:T(8,128)S(1)}, f32[8,66,1,128]{3,0,2,1:T(8,128)S(1)}, u32[]{:S(2)}, u32[]{:S(2)}) %collective-permute-start.10) | collective-permute-done | bytes 270368 | tf_op jit(solution)/shard_map/ppermute | solution.py:18
  47.4 7.2 %collective-permute-done.11 = f32[8,66,1,128]{3,0,2,1:T(8,128)S(1)} collective-permute-done((f32[8,66,1,128]{3,0,2,1:T(8,128)S(1)}, f32[8,66,1,128]{3,0,2,1:T(8,128)S(1)}, u32[]{:S(2)}, u32[]{:S(2)}) %collective-permute-start.11) | collective-permute-done | bytes 270368 | tf_op jit(solution)/shard_map/ppermute | solution.py:15
  54.6 7.5 %multiply_subtract_fusion = (f32[8,64,16,128]{3,0,2,1:T(8,128)S(1)}, f32[8,64,16,128]{3,0,2,1:T(8,128)S(1)}) fusion(f32[8,64,16]{0,2,1:T(8,128)S(1)} %fusion.43, f32[64,16,128]{2,1,0:T(8,128)S(1)} %get-tuple-element.9, f32[64,16,128]{2,1,0:T(8,128)S(1)} %pad.18, f32[8,64,16,128]{3,0,2,1:T(8,128)S(1)} %broadcast_multiply_fusion, ...), kind=kLoop, calls=%fused_computation.51 | loop fusion | flops 25165824 | bytes 17481728 | tf_op jit(solution)/shard_map/sub | solution.py:73
  62.1 1.3 collective-permute-start.12
  63.4 3.0 %collective-permute-start.13 = (f32[8,1,16,128]{3,0,2,1:T(8,128)S(1)}, f32[8,1,16,128]{3,0,2,1:T(8,128)S(1)}, u32[]{:S(2)}, u32[]{:S(2)}) collective-permute-start(f32[8,1,16,128]{3,0,2,1:T(8,128)S(1)} %get-tuple-element.15), channel_id=1, source_target_pairs={{0,8},{8,16},{16,24},{1,9},{9,17},{17,25},{2,10},{10,18},{18,26},{... | collective-permute-start | bytes 196616 | tf_op jit(solution)/shard_map/ppermute | solution.py:15
  66.5 0.9 collective-permute-done.13
  67.4 1.3 collective-permute-start.14
  68.7 5.0 %collective-permute-start.15 = (f32[8,66,1,128]{3,0,2,1:T(8,128)S(1)}, f32[8,66,1,128]{3,0,2,1:T(8,128)S(1)}, u32[]{:S(2)}, u32[]{:S(2)}) collective-permute-start(f32[8,66,1,128]{3,0,2,1:T(8,128)S(1)} %get-tuple-element.12), channel_id=1, source_target_pairs={{0,1},{1,2},{2,3},{3,4},{4,5},{5,6},{6,7},{8,9},{9,10},{10,11},{11... | collective-permute-start | bytes 811016 | tf_op jit(solution)/shard_map/ppermute | solution.py:15
  73.7 11.2 %fusion.28 = f32[16,16]{0,1:T(8,128)S(1)} fusion(f32[8,64,16,128]{3,0,2,1:T(8,128)S(1)} %get-tuple-element.7, f32[8,64,16,128]{3,0,2,1:T(8,128)S(1)} %broadcast_multiply_fusion), kind=kOutput, calls=%fused_computation.55 | convolution fusion | flops 404750336 | bytes 8389632 | tf_op jit(solution)/shard_map/aijk,bijk->ab/dot_general | solution.py:78
  84.9 0.4 collective-permute-done.15
  85.3 6.8 %fusion.10 = f32[8,64,16,128]{3,0,2,1:T(8,128)S(1)} fusion(f32[8,64,16,128]{3,0,2,1:T(8,128)S(1)} %get-tuple-element.7, f32[8,66,1,128]{3,0,2,1:T(8,128)S(1)} %collective-permute-done.15, f32[8,1,16,128]{3,0,2,1:T(8,128)S(1)} %collective-permute-done.12, f32[8,1,16,128]{3,0,2,1:T(8,128)S(1)} %collective-permute-done.13, ...), kind=kLoop, calls=%fused_computation.16 | loop fusion | flops 22020096 | bytes 12730368 | tf_op jit(solution)/shard_map/sub | solution.py:39
  92.1 1.9 %copy-done.5 = f32[8,64,16,128]{3,0,2,1:T(8,128)} copy-done((f32[8,64,16,128]{3,0,2,1:T(8,128)}, f32[8,64,16,128]{3,0,2,1:T(8,128)S(1)}, u32[]{:S(2)}) %copy-start.5) | copy-done | bytes 4194328
  94.1 10.4 %fusion.29 = f32[16,16]{1,0:T(8,128)S(1)} fusion(f32[8,64,16,128]{3,0,2,1:T(8,128)S(1)} %fusion.10, f32[8,64,16,128]{3,0,2,1:T(8,128)S(1)} %get-tuple-element.8, f32[8,64,16,128]{3,0,2,1:T(8,128)S(1)} %get-tuple-element.7, f32[8,64,16,128]{3,0,2,1:T(8,128)S(1)} %broadcast_multiply_fusion), kind=kOutput, calls=%fused_computation.56 | convolution fusion | flops 406847488 | bytes 16778240 | tf_op jit(solution)/shard_map/aijk,bijk->ab/dot_general | solution.py:79
  104.5 44.6 %all-reduce.4 = (f32[16,16]{0,1:T(8,128)S(1)}, f32[16,16]{1,0:T(8,128)S(1)}) all-reduce(f32[16,16]{0,1:T(8,128)S(1)} %fusion.28, f32[16,16]{1,0:T(8,128)S(1)} %fusion.29), channel_id=1, replica_groups=mesh['gx'=4,'gy'=8] {'gx','gy'}, use_global_device_ids=true, to_apply=%region_1.2 | all-reduce | flops 512 | bytes 4096 | tf_op jit(solution)/shard_map/psum | solution.py:80
  149.1 1.5 cholesky.44
  150.6 0.6 compare_reduce_fusion.1
  151.3 0.6 fusion.44
  151.9 1.2 custom-call.10
  153.1 0.2 fusion.52
  153.9 1.5 cholesky.55
  155.4 0.6 compare_reduce_fusion
  156.1 0.6 fusion.45
  156.7 1.2 custom-call.11
  157.9 0.2 fusion.48
  158.3 0.2 fusion.68
  158.5 6.6 %fusion = f32[1,64,16,128]{3,0,2,1:T(1,128)S(1)} fusion(f32[8,64,16,128]{3,0,2,1:T(8,128)} %copy-done.5, f32[8,64,16,128]{3,0,2,1:T(8,128)} %copy-done.4, f32[16]{0:T(128)S(1)} %get-tuple-element.25), kind=kOutput, calls=%fused_computation.6 | convolution fusion | flops 27262976 | bytes 8912960 | tf_op jit(solution)/shard_map/a,aijk->ijk/dot_general | solution.py:85
  165.1 0.9 sub.83
  166.0 8.6 %copy_add_fusion = f32[8,64,16,128]{3,0,2,1:T(8,128)S(1)} fusion(f32[8,64,16,128]{3,2,1,0:T(8,128)} %param.13, f32[8,64,16,128]{3,0,2,1:T(8,128)S(1)} %copy-done.3, f32[8,64,16,128]{3,0,2,1:T(8,128)S(1)} %copy-done.1, f32[16,8]{0,1:T(8,128)S(1)} %get-tuple-element.26), kind=kOutput, calls=%fused_computation.50 | convolution fusion | flops 204472320 | bytes 16777728 | tf_op jit(solution)/shard_map/ab,aijk->bijk/dot_general | solution.py:83
  174.6 2.8 %copy.15 = f32[8,64,16,128]{3,2,1,0:T(8,128)} copy(f32[8,64,16,128]{3,0,2,1:T(8,128)S(1)} %copy_add_fusion) | data formatting | bytes 8388608
  (57 shorter events, 1.3 us)
Async XLA Ops:
  0.6 7.1 %copy-start.7 = (f32[64,16,128]{2,1,0:T(8,128)S(1)}, f32[64,16,128]{2,1,0:T(8,128)}, u32[]{:S(2)}) copy-start(f32[64,16,128]{2,1,0:T(8,128)} %param.11) | copy-start | bytes 1572868
  0.6 12.9 %copy-start.8 = (f32[64,16,128]{2,1,0:T(8,128)S(1)}, f32[64,16,128]{2,1,0:T(8,128)}, u32[]{:S(2)}) copy-start(f32[64,16,128]{2,1,0:T(8,128)} %param.10) | copy-start | bytes 1572868
  0.7 15.9 %copy-start.10 = (s32[64,16]{0,1:T(8,128)S(1)}, s32[64,16]{0,1:T(8,128)}, u32[]{:S(2)}) copy-start(s32[64,16]{0,1:T(8,128)} %param.14) | copy-start | bytes 12292
  0.7 28.0 %copy-start.6 = (f32[64,16,128]{2,1,0:T(8,128)S(1)}, f32[64,16,128]{2,1,0:T(8,128)}, u32[]{:S(2)}) copy-start(f32[64,16,128]{2,1,0:T(8,128)} %param.12) | copy-start | bytes 1572868
  0.7 28.0 %copy-start.9 = (f32[64,16,128]{2,1,0:T(8,128)S(1)}, f32[64,16,128]{2,1,0:T(8,128)}, u32[]{:S(2)}) copy-start(f32[64,16,128]{2,1,0:T(8,128)} %param.9) | copy-start | bytes 1572868
  3.4 13.3 %collective-permute-start = (f32[1,16,128]{2,1,0:T(8,128)S(1)}, f32[1,16,128]{2,1,0:T(8,128)S(1)}, u32[]{:S(2)}, u32[]{:S(2)}) collective-permute-start(f32[1,16,128]{2,1,0:T(8,128)S(1)} %get-tuple-element.24), channel_id=1, source_target_pairs={{8,0},{16,8},{24,16},{9,1},{17,9},{25,17},{10,2},{18,10},{26,18},{... | collective-permute-start | bytes 24584 | tf_op jit(solution)/shard_map/ppermute | solution.py:18
  4.7 12.0 %collective-permute-start.2 = (f32[1,16,128]{2,1,0:T(8,128)S(1)}, f32[1,16,128]{2,1,0:T(8,128)S(1)}, u32[]{:S(2)}, u32[]{:S(2)}) collective-permute-start(f32[1,16,128]{2,1,0:T(8,128)S(1)} %get-tuple-element.23), channel_id=1, source_target_pairs={{0,8},{8,16},{16,24},{1,9},{9,17},{17,25},{2,10},{10,18},{18,26},{... | collective-permute-start | bytes 24584 | tf_op jit(solution)/shard_map/ppermute | solution.py:15
  7.7 14.9 %collective-permute-start.4 = (f32[1,16,128]{2,1,0:T(8,128)S(1)}, f32[1,16,128]{2,1,0:T(8,128)S(1)}, u32[]{:S(2)}, u32[]{:S(2)}) collective-permute-start(f32[1,16,128]{2,1,0:T(8,128)S(1)} %get-tuple-element.22), channel_id=1, source_target_pairs={{0,8},{8,16},{16,24},{1,9},{9,17},{17,25},{2,10},{10,18},{18,26},{... | collective-permute-start | bytes 24584 | tf_op jit(solution)/shard_map/ppermute | solution.py:15
  12.2 10.4 %collective-permute-start.5 = (f32[1,16,128]{2,1,0:T(8,128)S(1)}, f32[1,16,128]{2,1,0:T(8,128)S(1)}, u32[]{:S(2)}, u32[]{:S(2)}) collective-permute-start(f32[1,16,128]{2,1,0:T(8,128)S(1)} %get-tuple-element.21), channel_id=1, source_target_pairs={{8,0},{16,8},{24,16},{9,1},{17,9},{25,17},{10,2},{18,10},{26,18},{... | collective-permute-start | bytes 24584 | tf_op jit(solution)/shard_map/ppermute | solution.py:18
  13.6 13.7 %collective-permute-start.1 = (f32[1,16,128]{2,1,0:T(8,128)S(1)}, f32[1,16,128]{2,1,0:T(8,128)S(1)}, u32[]{:S(2)}, u32[]{:S(2)}) collective-permute-start(f32[1,16,128]{2,1,0:T(8,128)S(1)} %slice.156), channel_id=1, source_target_pairs={{0,8},{8,16},{16,24},{1,9},{9,17},{17,25},{2,10},{10,18},{18,26},{... | collective-permute-start | bytes 24584 | tf_op jit(solution)/shard_map/ppermute | solution.py:15
  16.8 10.5 %collective-permute-start.3 = (f32[66,1,128]{2,1,0:T(1,128)S(1)}, f32[66,1,128]{2,1,0:T(1,128)S(1)}, u32[]{:S(2)}, u32[]{:S(2)}) collective-permute-start(f32[66,1,128]{2,1,0:T(1,128)S(1)} %get-tuple-element.19), channel_id=1, source_target_pairs={{1,0},{2,1},{3,2},{4,3},{5,4},{6,5},{7,6},{9,8},{10,9},{11,10},{12... | collective-permute-start | bytes 101384 | tf_op jit(solution)/shard_map/ppermute | solution.py:18
  18.1 9.2 %collective-permute-start.7 = (f32[66,1,128]{2,1,0:T(1,128)S(1)}, f32[66,1,128]{2,1,0:T(1,128)S(1)}, u32[]{:S(2)}, u32[]{:S(2)}) collective-permute-start(f32[66,1,128]{2,1,0:T(1,128)S(1)} %get-tuple-element.20), channel_id=1, source_target_pairs={{0,1},{1,2},{2,3},{3,4},{4,5},{5,6},{6,7},{8,9},{9,10},{10,11},{11... | collective-permute-start | bytes 101384 | tf_op jit(solution)/shard_map/ppermute | solution.py:15
  22.7 5.9 %collective-permute-start.6 = (f32[66,1,128]{2,1,0:T(1,128)S(1)}, f32[66,1,128]{2,1,0:T(1,128)S(1)}, u32[]{:S(2)}, u32[]{:S(2)}) collective-permute-start(f32[66,1,128]{2,1,0:T(1,128)S(1)} %slice.194), channel_id=1, source_target_pairs={{0,1},{1,2},{2,3},{3,4},{4,5},{5,6},{6,7},{8,9},{9,10},{10,11},{11... | collective-permute-start | bytes 101384 | tf_op jit(solution)/shard_map/ppermute | solution.py:15
  31.5 60.6 %copy-start = (f32[8,64,16,128]{3,0,2,1:T(8,128)}, f32[8,64,16,128]{3,0,2,1:T(8,128)S(1)}, u32[]{:S(2)}) copy-start(f32[8,64,16,128]{3,0,2,1:T(8,128)S(1)} %broadcast_multiply_fusion) | copy-start | bytes 12582916
  31.5 4.3 %collective-permute-start.8 = (f32[8,1,16,128]{3,0,2,1:T(8,128)S(1)}, f32[8,1,16,128]{3,0,2,1:T(8,128)S(1)}, u32[]{:S(2)}, u32[]{:S(2)}) collective-permute-start(f32[8,1,16,128]{3,0,2,1:T(8,128)S(1)} %get-tuple-element.18), channel_id=1, source_target_pairs={{8,0},{16,8},{24,16},{9,1},{17,9},{25,17},{10,2},{18,10},{26,18},{... | collective-permute-start | bytes 196616 | tf_op jit(solution)/shard_map/ppermute | solution.py:18
  32.8 3.9 %collective-permute-start.9 = (f32[8,1,16,128]{3,0,2,1:T(8,128)S(1)}, f32[8,1,16,128]{3,0,2,1:T(8,128)S(1)}, u32[]{:S(2)}, u32[]{:S(2)}) collective-permute-start(f32[8,1,16,128]{3,0,2,1:T(8,128)S(1)} %get-tuple-element.17), channel_id=1, source_target_pairs={{0,8},{8,16},{16,24},{1,9},{9,17},{17,25},{2,10},{10,18},{18,26},{... | collective-permute-start | bytes 196616 | tf_op jit(solution)/shard_map/ppermute | solution.py:15
  36.8 10.6 %collective-permute-start.10 = (f32[8,66,1,128]{3,0,2,1:T(8,128)S(1)}, f32[8,66,1,128]{3,0,2,1:T(8,128)S(1)}, u32[]{:S(2)}, u32[]{:S(2)}) collective-permute-start(f32[8,66,1,128]{3,0,2,1:T(8,128)S(1)} %get-tuple-element.13), channel_id=1, source_target_pairs={{1,0},{2,1},{3,2},{4,3},{5,4},{6,5},{7,6},{9,8},{10,9},{11,10},{12... | collective-permute-start | bytes 811016 | tf_op jit(solution)/shard_map/ppermute | solution.py:18
  38.1 16.6 %collective-permute-start.11 = (f32[8,66,1,128]{3,0,2,1:T(8,128)S(1)}, f32[8,66,1,128]{3,0,2,1:T(8,128)S(1)}, u32[]{:S(2)}, u32[]{:S(2)}) collective-permute-start(f32[8,66,1,128]{3,0,2,1:T(8,128)S(1)} %get-tuple-element.14), channel_id=1, source_target_pairs={{0,1},{1,2},{2,3},{3,4},{4,5},{5,6},{6,7},{8,9},{9,10},{10,11},{11... | collective-permute-start | bytes 811016 | tf_op jit(solution)/shard_map/ppermute | solution.py:15
  62.1 30.0 %copy-start.2 = (f32[8,64,16,128]{3,0,2,1:T(8,128)}, f32[8,64,16,128]{3,0,2,1:T(8,128)S(1)}, u32[]{:S(2)}) copy-start(f32[8,64,16,128]{3,0,2,1:T(8,128)S(1)} %get-tuple-element.7) | copy-start | bytes 12582916
  62.1 30.0 %copy-start.4 = (f32[8,64,16,128]{3,0,2,1:T(8,128)}, f32[8,64,16,128]{3,0,2,1:T(8,128)S(1)}, u32[]{:S(2)}) copy-start(f32[8,64,16,128]{3,0,2,1:T(8,128)S(1)} %get-tuple-element.8) | copy-start | bytes 12582916
  62.1 4.3 %collective-permute-start.12 = (f32[8,1,16,128]{3,0,2,1:T(8,128)S(1)}, f32[8,1,16,128]{3,0,2,1:T(8,128)S(1)}, u32[]{:S(2)}, u32[]{:S(2)}) collective-permute-start(f32[8,1,16,128]{3,0,2,1:T(8,128)S(1)} %get-tuple-element.16), channel_id=1, source_target_pairs={{8,0},{16,8},{24,16},{9,1},{17,9},{25,17},{10,2},{18,10},{26,18},{... | collective-permute-start | bytes 196616 | tf_op jit(solution)/shard_map/ppermute | solution.py:18
  63.4 3.9 %collective-permute-start.13 = (f32[8,1,16,128]{3,0,2,1:T(8,128)S(1)}, f32[8,1,16,128]{3,0,2,1:T(8,128)S(1)}, u32[]{:S(2)}, u32[]{:S(2)}) collective-permute-start(f32[8,1,16,128]{3,0,2,1:T(8,128)S(1)} %get-tuple-element.15), channel_id=1, source_target_pairs={{0,8},{8,16},{16,24},{1,9},{9,17},{17,25},{2,10},{10,18},{18,26},{... | collective-permute-start | bytes 196616 | tf_op jit(solution)/shard_map/ppermute | solution.py:15
  67.4 17.5 %collective-permute-start.14 = (f32[8,66,1,128]{3,0,2,1:T(8,128)S(1)}, f32[8,66,1,128]{3,0,2,1:T(8,128)S(1)}, u32[]{:S(2)}, u32[]{:S(2)}) collective-permute-start(f32[8,66,1,128]{3,0,2,1:T(8,128)S(1)} %get-tuple-element.11), channel_id=1, source_target_pairs={{1,0},{2,1},{3,2},{4,3},{5,4},{6,5},{7,6},{9,8},{10,9},{11,10},{12... | collective-permute-start | bytes 811016 | tf_op jit(solution)/shard_map/ppermute | solution.py:18
  68.7 16.6 %collective-permute-start.15 = (f32[8,66,1,128]{3,0,2,1:T(8,128)S(1)}, f32[8,66,1,128]{3,0,2,1:T(8,128)S(1)}, u32[]{:S(2)}, u32[]{:S(2)}) collective-permute-start(f32[8,66,1,128]{3,0,2,1:T(8,128)S(1)} %get-tuple-element.12), channel_id=1, source_target_pairs={{0,1},{1,2},{2,3},{3,4},{4,5},{5,6},{6,7},{8,9},{9,10},{10,11},{11... | collective-permute-start | bytes 811016 | tf_op jit(solution)/shard_map/ppermute | solution.py:15
  92.1 2.0 %copy-start.5 = (f32[8,64,16,128]{3,0,2,1:T(8,128)}, f32[8,64,16,128]{3,0,2,1:T(8,128)S(1)}, u32[]{:S(2)}) copy-start(f32[8,64,16,128]{3,0,2,1:T(8,128)S(1)} %fusion.10) | copy-start | bytes 12582916
  158.5 7.5 %copy-start.1 = (f32[8,64,16,128]{3,0,2,1:T(8,128)S(1)}, f32[8,64,16,128]{3,0,2,1:T(8,128)}, u32[]{:S(2)}) copy-start(f32[8,64,16,128]{3,0,2,1:T(8,128)} %copy-done) | copy-start | bytes 12582916
  158.5 7.5 %copy-start.3 = (f32[8,64,16,128]{3,0,2,1:T(8,128)S(1)}, f32[8,64,16,128]{3,0,2,1:T(8,128)}, u32[]{:S(2)}) copy-start(f32[8,64,16,128]{3,0,2,1:T(8,128)} %copy-done.2) | copy-start | bytes 12582916
where the time goes:
time: 178 us; the launch traced here: 177 us
  starting transfers between devices  44.6 us (25%)
  blocking collectives  44.6 us (25%)
  matrix products  37.9 us (21%)
  other arithmetic  29 us (16%)
  waiting for transfers between devices  14.8 us (8%)
  local copies, waits for them, and re-layouts  5.36 us (3%)
    psum x1, blocking collectives, shards(): gram = lax.psum(gram_local, ('gx', 'gy'))  44.6 us
    ppermute x9, starting transfers between devices, padded_2(): lax.ppermute(lax.slice_in_dim(block, block.shape[dim] - width, None, axis...  35.5 us
    dot_general x1, matrix products, shards(): gram_local = jnp.einsum('aijk,bijk->ab', basis, basis, precision=highest)  11.2 us
    ppermute x9, waiting for transfers between devices, padded_2(): lax.ppermute(lax.slice_in_dim(block, block.shape[dim] - width, None, axis...  10.7 us
    dot_general x1, matrix products, shards(): project_local = jnp.einsum('aijk,bijk->ab', basis, image, precision=highest)  10.4 us
    ppermute x7, starting transfers between devices, padded_2(): lax.ppermute(lax.slice_in_dim(block, 0, width, axis=dim), axis, backward)  9.04 us
    dot_general x1, matrix products, shards(): jnp.einsum('ab,aijk->bijk', coeffs, basis, precision=highest)  8.56 us
    sub x1, other arithmetic, shards(): powered = applied - basis_shift * blocks  7.45 us
  transfers between devices with their start and end apart: 16, of which 6 were waited for; matrix products, arithmetic and copies ran while one was open for 7% of the time, Pallas kernels for 0%

commit v1 on v0

--- a/solution.py
+++ b/solution.py
@@ -77,7 +77,7 @@
     image = jnp.concatenate([applied, second], axis=0)
     gram_local = jnp.einsum("aijk,bijk->ab", basis, basis, precision=highest)
     project_local = jnp.einsum("aijk,bijk->ab", basis, image, precision=highest)
-    gram = lax.psum(gram_local, ("gx", "gy"))
+    gram = lax.psum(lax.psum(gram_local, "gy"), "gx")
     project = lax.psum(project_local, ("gx", "gy"))
     coeffs = finish(gram, project)
     new_iterates = iterates + jnp.einsum("ab,aijk->bijk", coeffs, basis, precision=highest)

time: 178 us -> 208 us (1.17)
  blocking collectives: 44.6 us -> 64.8 us
  waiting for transfers between devices: 14.8 us -> 20.8 us
  other arithmetic: 29 us -> 32.1 us
    psum x1 -> x3, blocking collectives: 44.6 us -> 64.8 us  [the longest x1 38.9 us: shards(): project = lax.psum(project_local, ('gx', 'gy'))]
    ppermute x7, waiting for transfers between devices: 4.06 us -> 7.78 us  [padded_2(): lax.ppermute(lax.slice_in_dim(block, 0, width, axis=dim), axis, backward)]
    ppermute x9, waiting for transfers between devices: 10.7 us -> 13.1 us  [padded_2(): lax.ppermute(lax.slice_in_dim(block, block.shape[dim] - width, None, axis...]
    unnamed x26 -> x36, local copies, waits for them, and re-layouts: 4.88 us -> 4.92 us
  transfers between devices with their start and end apart: 16 -> 16, of which waited for: 6 -> 6; matrix products, arithmetic and copies ran while one was open for 7% -> 2% of each run, Pallas kernels for 0% -> 0%
where the time goes in v1:
time: 208 us; the launch traced here: 207 us
  blocking collectives  64.8 us (31%)
  starting transfers between devices  44.6 us (21%)
  matrix products  38.1 us (18%)
  other arithmetic  32.1 us (15%)
  waiting for transfers between devices  20.8 us (10%)
  local copies, waits for them, and re-layouts  5.41 us (3%)
    psum x1, blocking collectives, shards(): project = lax.psum(project_local, ('gx', 'gy'))  38.9 us
    ppermute x9, starting transfers between devices, padded_2(): lax.ppermute(lax.slice_in_dim(block, block.shape[dim] - width, None, axis...  35.1 us
    psum x2, blocking collectives, shards(): gram = lax.psum(lax.psum(gram_local, 'gy'), 'gx')  25.9 us
    ppermute x9, waiting for transfers between devices, padded_2(): lax.ppermute(lax.slice_in_dim(block, block.shape[dim] - width, None, axis...  13.1 us
    dot_general x1, matrix products, shards(): gram_local = jnp.einsum('aijk,bijk->ab', basis, basis, precision=highest)  11.2 us
    dot_general x1, matrix products, shards(): project_local = jnp.einsum('aijk,bijk->ab', basis, image, precision=highest)  10.6 us
    ppermute x7, starting transfers between devices, padded_2(): lax.ppermute(lax.slice_in_dim(block, 0, width, axis=dim), axis, backward)  9.5 us
    dot_general x1, matrix products, shards(): jnp.einsum('ab,aijk->bijk', coeffs, basis, precision=highest)  8.55 us
  transfers between devices with their start and end apart: 16, of which 6 were waited for; matrix products, arithmetic and copies ran while one was open for 2% of the time, Pallas kernels for 0%

profile of v1, /device:TPU:0, one launch (start us, length us, event | category | flops | bytes accessed | tf_op | source)
XLA Modules:
  0.0 206.9 jit_solution(9376727739147043314)
XLA Ops:
  0.7 2.7 %reduce_sum.18 = f32[64,16,128]{2,1,0:T(8,128)S(1)} reduce(f32[8,64,16,128]{3,2,1,0:T(8,128)} %param.13, f32[]{:T(128)} %constant.43.clone.1), dimensions={0}, to_apply=%region_0.0 | reduce | flops 917504 | bytes 4718596 | tf_op jit(solution)/shard_map/reduce_sum | solution.py:60
  3.4 1.3 collective-permute-start
  4.7 3.0 %collective-permute-start.2 = (f32[1,16,128]{2,1,0:T(8,128)S(1)}, f32[1,16,128]{2,1,0:T(8,128)S(1)}, u32[]{:S(2)}, u32[]{:S(2)}) collective-permute-start(f32[1,16,128]{2,1,0:T(8,128)S(1)} %get-tuple-element.21), channel_id=1, source_target_pairs={{0,8},{8,16},{16,24},{1,9},{9,17},{17,25},{2,10},{10,18},{18,26},{... | collective-permute-start | bytes 24584 | tf_op jit(solution)/shard_map/ppermute | solution.py:15
  7.7 4.5 %collective-permute-start.4 = (f32[1,16,128]{2,1,0:T(8,128)S(1)}, f32[1,16,128]{2,1,0:T(8,128)S(1)}, u32[]{:S(2)}, u32[]{:S(2)}) collective-permute-start(f32[1,16,128]{2,1,0:T(8,128)S(1)} %get-tuple-element.20), channel_id=1, source_target_pairs={{0,8},{8,16},{16,24},{1,9},{9,17},{17,25},{2,10},{10,18},{18,26},{... | collective-permute-start | bytes 24584 | tf_op jit(solution)/shard_map/ppermute | solution.py:15
  12.2 1.3 collective-permute-start.5
  13.6 3.0 %collective-permute-start.1 = (f32[1,16,128]{2,1,0:T(8,128)S(1)}, f32[1,16,128]{2,1,0:T(8,128)S(1)}, u32[]{:S(2)}, u32[]{:S(2)}) collective-permute-start(f32[1,16,128]{2,1,0:T(8,128)S(1)} %slice.156), channel_id=1, source_target_pairs={{0,8},{8,16},{16,24},{1,9},{9,17},{17,25},{2,10},{10,18},{18,26},{... | collective-permute-start | bytes 24584 | tf_op jit(solution)/shard_map/ppermute | solution.py:15
  16.8 1.3 collective-permute-start.3
  18.1 4.5 %collective-permute-start.7 = (f32[66,1,128]{2,1,0:T(1,128)S(1)}, f32[66,1,128]{2,1,0:T(1,128)S(1)}, u32[]{:S(2)}, u32[]{:S(2)}) collective-permute-start(f32[66,1,128]{2,1,0:T(1,128)S(1)} %get-tuple-element.18), channel_id=1, source_target_pairs={{0,1},{1,2},{2,3},{3,4},{4,5},{5,6},{6,7},{8,9},{9,10},{10,11},{11... | collective-permute-start | bytes 101384 | tf_op jit(solution)/shard_map/ppermute | solution.py:15
  22.7 4.3 %collective-permute-start.6 = (f32[66,1,128]{2,1,0:T(1,128)S(1)}, f32[66,1,128]{2,1,0:T(1,128)S(1)}, u32[]{:S(2)}, u32[]{:S(2)}) collective-permute-start(f32[66,1,128]{2,1,0:T(1,128)S(1)} %slice.194), channel_id=1, source_target_pairs={{0,1},{1,2},{2,3},{3,4},{4,5},{5,6},{6,7},{8,9},{9,10},{10,11},{11... | collective-permute-start | bytes 101384 | tf_op jit(solution)/shard_map/ppermute | solution.py:15
  27.3 1.3 collective-permute-done.6
  28.6 1.6 fusion.33
  30.2 1.3 broadcast_multiply_fusion
  31.5 1.4 collective-permute-start.8
  33.0 3.0 %collective-permute-start.9 = (f32[8,1,16,128]{3,0,2,1:T(8,128)S(1)}, f32[8,1,16,128]{3,0,2,1:T(8,128)S(1)}, u32[]{:S(2)}, u32[]{:S(2)}) collective-permute-start(f32[8,1,16,128]{3,0,2,1:T(8,128)S(1)} %get-tuple-element.15), channel_id=1, source_target_pairs={{0,8},{8,16},{16,24},{1,9},{9,17},{17,25},{2,10},{10,18},{18,26},{... | collective-permute-start | bytes 196616 | tf_op jit(solution)/shard_map/ppermute | solution.py:15
  36.0 0.9 collective-permute-done.9
  36.9 1.3 collective-permute-start.10
  38.2 5.0 %collective-permute-start.11 = (f32[8,66,1,128]{3,0,2,1:T(8,128)S(1)}, f32[8,66,1,128]{3,0,2,1:T(8,128)S(1)}, u32[]{:S(2)}, u32[]{:S(2)}) collective-permute-start(f32[8,66,1,128]{3,0,2,1:T(8,128)S(1)} %get-tuple-element.12), channel_id=1, source_target_pairs={{0,1},{1,2},{2,3},{3,4},{4,5},{5,6},{6,7},{8,9},{9,10},{10,11},{11... | collective-permute-start | bytes 811016 | tf_op jit(solution)/shard_map/ppermute | solution.py:15
  43.5 4.0 %collective-permute-done.10 = f32[8,66,1,128]{3,0,2,1:T(8,128)S(1)} collective-permute-done((f32[8,66,1,128]{3,0,2,1:T(8,128)S(1)}, f32[8,66,1,128]{3,0,2,1:T(8,128)S(1)}, u32[]{:S(2)}, u32[]{:S(2)}) %collective-permute-start.10) | collective-permute-done | bytes 270368 | tf_op jit(solution)/shard_map/ppermute | solution.py:18
  47.6 7.2 %collective-permute-done.11 = f32[8,66,1,128]{3,0,2,1:T(8,128)S(1)} collective-permute-done((f32[8,66,1,128]{3,0,2,1:T(8,128)S(1)}, f32[8,66,1,128]{3,0,2,1:T(8,128)S(1)}, u32[]{:S(2)}, u32[]{:S(2)}) %collective-permute-start.11) | collective-permute-done | bytes 270368 | tf_op jit(solution)/shard_map/ppermute | solution.py:15
  54.8 8.3 %multiply_subtract_fusion = (f32[8,64,16,128]{3,0,2,1:T(8,128)S(1)}, f32[8,64,16,128]{3,0,2,1:T(8,128)}) fusion(f32[8,64,16]{0,2,1:T(8,128)S(1)} %fusion.43, f32[64,16,128]{2,1,0:T(8,128)S(1)} %get-tuple-element.7, f32[64,16,128]{2,1,0:T(8,128)S(1)} %pad.18, f32[8,64,16,128]{3,0,2,1:T(8,128)S(1)} %broadcast_multiply_fusion, f32[64,16,128]{2,1,0:T(8,128)S(1)} %copy-done.8, ...), kind=kLoop, calls=%fused_computation.51 | loop fusion | flops 25165824 | bytes 17481728 | tf_op jit(solution)/shard_map/sub | solution.py:73
  63.1 11.2 %fusion.28 = f32[16,16]{0,1:T(8,128)S(1)} fusion(f32[8,64,16,128]{3,0,2,1:T(8,128)S(1)} %get-tuple-element.5, f32[8,64,16,128]{3,0,2,1:T(8,128)S(1)} %broadcast_multiply_fusion), kind=kOutput, calls=%fused_computation.55 | convolution fusion | flops 404750336 | bytes 8389632 | tf_op jit(solution)/shard_map/aijk,bijk->ab/dot_general | solution.py:78
  74.3 1.3 collective-permute-start.12
  75.6 3.0 %collective-permute-start.13 = (f32[8,1,16,128]{3,0,2,1:T(8,128)S(1)}, f32[8,1,16,128]{3,0,2,1:T(8,128)S(1)}, u32[]{:S(2)}, u32[]{:S(2)}) collective-permute-start(f32[8,1,16,128]{3,0,2,1:T(8,128)S(1)} %get-tuple-element.13), channel_id=1, source_target_pairs={{0,8},{8,16},{16,24},{1,9},{9,17},{17,25},{2,10},{10,18},{18,26},{... | collective-permute-start | bytes 196616 | tf_op jit(solution)/shard_map/ppermute | solution.py:15
  78.6 20.1 %psum.21 = f32[16,16]{0,1:T(8,128)S(1)} all-reduce(f32[16,16]{0,1:T(8,128)S(1)} %fusion.28), channel_id=1, replica_groups=mesh['gx'=4,'gy'=8] {'gy'}, use_global_device_ids=true, to_apply=%region_1.2 | all-reduce | flops 256 | bytes 2048 | tf_op jit(solution)/shard_map/psum | solution.py:80
  98.8 5.8 %psum.22 = f32[16,16]{0,1:T(8,128)S(1)} all-reduce(f32[16,16]{0,1:T(8,128)S(1)} %psum.21), channel_id=1, replica_groups=mesh['gx'=4,'gy'=8] {'gx'}, use_global_device_ids=true, to_apply=%region_2.3 | all-reduce | flops 256 | bytes 2048 | tf_op jit(solution)/shard_map/psum | solution.py:80
  104.6 1.5 cholesky.44
  106.1 0.7 compare_reduce_fusion.1
  106.8 0.6 fusion.44
  107.4 1.2 custom-call.10
  108.6 1.2 pad_maximum_fusion.43
  109.9 1.6 collective-permute-start.14
  111.5 4.6 %collective-permute-start.15 = (f32[8,66,1,128]{3,0,2,1:T(8,128)S(1)}, f32[8,66,1,128]{3,0,2,1:T(8,128)S(1)}, u32[]{:S(2)}, u32[]{:S(2)}) collective-permute-start(f32[8,66,1,128]{3,0,2,1:T(8,128)S(1)} %get-tuple-element.10), channel_id=1, source_target_pairs={{0,1},{1,2},{2,3},{3,4},{4,5},{5,6},{6,7},{8,9},{9,10},{10,11},{11... | collective-permute-start | bytes 811016 | tf_op jit(solution)/shard_map/ppermute | solution.py:15
  116.4 3.7 %collective-permute-done.14 = f32[8,66,1,128]{3,0,2,1:T(8,128)S(1)} collective-permute-done((f32[8,66,1,128]{3,0,2,1:T(8,128)S(1)}, f32[8,66,1,128]{3,0,2,1:T(8,128)S(1)}, u32[]{:S(2)}, u32[]{:S(2)}) %collective-permute-start.14) | collective-permute-done | bytes 270368 | tf_op jit(solution)/shard_map/ppermute | solution.py:18
  120.1 3.6 %collective-permute-done.15 = f32[8,66,1,128]{3,0,2,1:T(8,128)S(1)} collective-permute-done((f32[8,66,1,128]{3,0,2,1:T(8,128)S(1)}, f32[8,66,1,128]{3,0,2,1:T(8,128)S(1)}, u32[]{:S(2)}, u32[]{:S(2)}) %collective-permute-start.15) | collective-permute-done | bytes 270368 | tf_op jit(solution)/shard_map/ppermute | solution.py:15
  123.7 7.9 %fusion.10 = f32[8,64,16,128]{3,0,2,1:T(8,128)S(1)} fusion(f32[8,64,16,128]{3,0,2,1:T(8,128)S(1)} %copy-done.4, f32[8,66,1,128]{3,0,2,1:T(8,128)S(1)} %collective-permute-done.15, f32[8,1,16,128]{3,0,2,1:T(8,128)S(1)} %collective-permute-done.12, f32[8,1,16,128]{3,0,2,1:T(8,128)S(1)} %collective-permute-done.13, ...), kind=kLoop, calls=%fused_computation.16 | loop fusion | flops 22020096 | bytes 12730368 | tf_op jit(solution)/shard_map/sub | solution.py:39
  131.6 2.0 copy-done.7
  133.5 10.6 %fusion.29 = f32[16,16]{1,0:T(8,128)S(1)} fusion(f32[8,64,16,128]{3,0,2,1:T(8,128)S(1)} %fusion.10, f32[8,64,16,128]{3,0,2,1:T(8,128)S(1)} %copy-done.6, f32[8,64,16,128]{3,0,2,1:T(8,128)S(1)} %copy-done.4, f32[8,64,16,128]{3,0,2,1:T(8,128)S(1)} %copy-done.1), kind=kOutput, calls=%fused_computation.56 | convolution fusion | flops 406847488 | bytes 16778240 | tf_op jit(solution)/shard_map/aijk,bijk->ab/dot_general | solution.py:79
  144.2 38.9 %psum.23 = f32[16,16]{1,0:T(8,128)S(1)} all-reduce(f32[16,16]{1,0:T(8,128)S(1)} %fusion.29), channel_id=1, replica_groups=mesh['gx'=4,'gy'=8] {'gx','gy'}, use_global_device_ids=true, to_apply=%region_5.7 | all-reduce | flops 256 | bytes 2048 | tf_op jit(solution)/shard_map/psum | solution.py:81
  183.5 1.5 cholesky.55
  185.0 0.6 compare_reduce_fusion
  185.7 0.6 fusion.45
  186.3 1.2 custom-call.11
  187.5 0.2 fusion.48
  187.9 0.2 fusion.68
  188.1 6.6 %fusion = f32[1,64,16,128]{3,0,2,1:T(1,128)S(1)} fusion(f32[8,64,16,128]{3,0,2,1:T(8,128)} %copy-done.7, f32[8,64,16,128]{3,0,2,1:T(8,128)} %get-tuple-element.6, f32[16]{0:T(128)S(1)} %get-tuple-element.23), kind=kOutput, calls=%fused_computation.6 | convolution fusion | flops 27262976 | bytes 8912960 | tf_op jit(solution)/shard_map/a,aijk->ijk/dot_general | solution.py:85
  194.7 0.9 sub.83
  195.6 8.6 %copy_add_fusion = f32[8,64,16,128]{3,0,2,1:T(8,128)S(1)} fusion(f32[8,64,16,128]{3,2,1,0:T(8,128)} %param.13, f32[8,64,16,128]{3,0,2,1:T(8,128)S(1)} %copy-done.5, f32[8,64,16,128]{3,0,2,1:T(8,128)S(1)} %copy-done.2, f32[16,8]{0,1:T(8,128)S(1)} %get-tuple-element.24), kind=kOutput, calls=%fused_computation.50 | convolution fusion | flops 204472320 | bytes 16777728 | tf_op jit(solution)/shard_map/ab,aijk->bijk/dot_general | solution.py:83
  204.2 2.8 %copy.15 = f32[8,64,16,128]{3,2,1,0:T(8,128)} copy(f32[8,64,16,128]{3,0,2,1:T(8,128)S(1)} %copy_add_fusion) | data formatting | bytes 8388608
  (69 shorter events, 1.8 us)
Async XLA Ops:
  0.6 7.1 %copy-start.9 = (f32[64,16,128]{2,1,0:T(8,128)S(1)}, f32[64,16,128]{2,1,0:T(8,128)}, u32[]{:S(2)}) copy-start(f32[64,16,128]{2,1,0:T(8,128)} %param.11) | copy-start | bytes 1572868
  0.6 12.9 %copy-start.10 = (f32[64,16,128]{2,1,0:T(8,128)S(1)}, f32[64,16,128]{2,1,0:T(8,128)}, u32[]{:S(2)}) copy-start(f32[64,16,128]{2,1,0:T(8,128)} %param.10) | copy-start | bytes 1572868
  0.7 16.0 %copy-start.15 = (s32[64,16]{0,1:T(8,128)S(1)}, s32[64,16]{0,1:T(8,128)}, u32[]{:S(2)}) copy-start(s32[64,16]{0,1:T(8,128)} %param.14) | copy-start | bytes 12292
  0.7 28.0 %copy-start.8 = (f32[64,16,128]{2,1,0:T(8,128)S(1)}, f32[64,16,128]{2,1,0:T(8,128)}, u32[]{:S(2)}) copy-start(f32[64,16,128]{2,1,0:T(8,128)} %param.12) | copy-start | bytes 1572868
  0.7 28.0 %copy-start.11 = (f32[64,16,128]{2,1,0:T(8,128)S(1)}, f32[64,16,128]{2,1,0:T(8,128)}, u32[]{:S(2)}) copy-start(f32[64,16,128]{2,1,0:T(8,128)} %param.9) | copy-start | bytes 1572868
  3.4 13.3 %collective-permute-start = (f32[1,16,128]{2,1,0:T(8,128)S(1)}, f32[1,16,128]{2,1,0:T(8,128)S(1)}, u32[]{:S(2)}, u32[]{:S(2)}) collective-permute-start(f32[1,16,128]{2,1,0:T(8,128)S(1)} %get-tuple-element.22), channel_id=1, source_target_pairs={{8,0},{16,8},{24,16},{9,1},{17,9},{25,17},{10,2},{18,10},{26,18},{... | collective-permute-start | bytes 24584 | tf_op jit(solution)/shard_map/ppermute | solution.py:18
  4.7 12.0 %collective-permute-start.2 = (f32[1,16,128]{2,1,0:T(8,128)S(1)}, f32[1,16,128]{2,1,0:T(8,128)S(1)}, u32[]{:S(2)}, u32[]{:S(2)}) collective-permute-start(f32[1,16,128]{2,1,0:T(8,128)S(1)} %get-tuple-element.21), channel_id=1, source_target_pairs={{0,8},{8,16},{16,24},{1,9},{9,17},{17,25},{2,10},{10,18},{18,26},{... | collective-permute-start | bytes 24584 | tf_op jit(solution)/shard_map/ppermute | solution.py:15
  7.7 14.9 %collective-permute-start.4 = (f32[1,16,128]{2,1,0:T(8,128)S(1)}, f32[1,16,128]{2,1,0:T(8,128)S(1)}, u32[]{:S(2)}, u32[]{:S(2)}) collective-permute-start(f32[1,16,128]{2,1,0:T(8,128)S(1)} %get-tuple-element.20), channel_id=1, source_target_pairs={{0,8},{8,16},{16,24},{1,9},{9,17},{17,25},{2,10},{10,18},{18,26},{... | collective-permute-start | bytes 24584 | tf_op jit(solution)/shard_map/ppermute | solution.py:15
  12.2 10.4 %collective-permute-start.5 = (f32[1,16,128]{2,1,0:T(8,128)S(1)}, f32[1,16,128]{2,1,0:T(8,128)S(1)}, u32[]{:S(2)}, u32[]{:S(2)}) collective-permute-start(f32[1,16,128]{2,1,0:T(8,128)S(1)} %get-tuple-element.19), channel_id=1, source_target_pairs={{8,0},{16,8},{24,16},{9,1},{17,9},{25,17},{10,2},{18,10},{26,18},{... | collective-permute-start | bytes 24584 | tf_op jit(solution)/shard_map/ppermute | solution.py:18
  13.6 13.7 %collective-permute-start.1 = (f32[1,16,128]{2,1,0:T(8,128)S(1)}, f32[1,16,128]{2,1,0:T(8,128)S(1)}, u32[]{:S(2)}, u32[]{:S(2)}) collective-permute-start(f32[1,16,128]{2,1,0:T(8,128)S(1)} %slice.156), channel_id=1, source_target_pairs={{0,8},{8,16},{16,24},{1,9},{9,17},{17,25},{2,10},{10,18},{18,26},{... | collective-permute-start | bytes 24584 | tf_op jit(solution)/shard_map/ppermute | solution.py:15
  16.8 10.5 %collective-permute-start.3 = (f32[66,1,128]{2,1,0:T(1,128)S(1)}, f32[66,1,128]{2,1,0:T(1,128)S(1)}, u32[]{:S(2)}, u32[]{:S(2)}) collective-permute-start(f32[66,1,128]{2,1,0:T(1,128)S(1)} %get-tuple-element.17), channel_id=1, source_target_pairs={{1,0},{2,1},{3,2},{4,3},{5,4},{6,5},{7,6},{9,8},{10,9},{11,10},{12... | collective-permute-start | bytes 101384 | tf_op jit(solution)/shard_map/ppermute | solution.py:18
  18.1 9.2 %collective-permute-start.7 = (f32[66,1,128]{2,1,0:T(1,128)S(1)}, f32[66,1,128]{2,1,0:T(1,128)S(1)}, u32[]{:S(2)}, u32[]{:S(2)}) collective-permute-start(f32[66,1,128]{2,1,0:T(1,128)S(1)} %get-tuple-element.18), channel_id=1, source_target_pairs={{0,1},{1,2},{2,3},{3,4},{4,5},{5,6},{6,7},{8,9},{9,10},{10,11},{11... | collective-permute-start | bytes 101384 | tf_op jit(solution)/shard_map/ppermute | solution.py:15
  22.7 5.9 %collective-permute-start.6 = (f32[66,1,128]{2,1,0:T(1,128)S(1)}, f32[66,1,128]{2,1,0:T(1,128)S(1)}, u32[]{:S(2)}, u32[]{:S(2)}) collective-permute-start(f32[66,1,128]{2,1,0:T(1,128)S(1)} %slice.194), channel_id=1, source_target_pairs={{0,1},{1,2},{2,3},{3,4},{4,5},{5,6},{6,7},{8,9},{9,10},{10,11},{11... | collective-permute-start | bytes 101384 | tf_op jit(solution)/shard_map/ppermute | solution.py:15
  30.2 24.6 %copy-start.14 = (f32[64,16,128]{2,1,0:T(8,128)}, f32[64,16,128]{2,1,0:T(8,128)S(1)}, u32[]{:S(2)}) copy-start(f32[64,16,128]{2,1,0:T(8,128)S(1)} %get-tuple-element.8) | copy-start | bytes 1572868
  31.5 31.6 %copy-start = (f32[8,64,16,128]{3,0,2,1:T(8,128)}, f32[8,64,16,128]{3,0,2,1:T(8,128)S(1)}, u32[]{:S(2)}) copy-start(f32[8,64,16,128]{3,0,2,1:T(8,128)S(1)} %broadcast_multiply_fusion) | copy-start | bytes 12582916
  31.5 23.3 %copy-start.12 = (f32[64,16,128]{2,1,0:T(8,128)S(1)}, f32[64,16,128]{2,1,0:T(8,128)}, u32[]{:S(2)}) copy-start(f32[64,16,128]{2,1,0:T(8,128)} %param.9) | copy-start | bytes 1572868
  31.5 4.5 %collective-permute-start.8 = (f32[8,1,16,128]{3,0,2,1:T(8,128)S(1)}, f32[8,1,16,128]{3,0,2,1:T(8,128)S(1)}, u32[]{:S(2)}, u32[]{:S(2)}) collective-permute-start(f32[8,1,16,128]{3,0,2,1:T(8,128)S(1)} %get-tuple-element.16), channel_id=1, source_target_pairs={{8,0},{16,8},{24,16},{9,1},{17,9},{25,17},{10,2},{18,10},{26,18},{... | collective-permute-start | bytes 196616 | tf_op jit(solution)/shard_map/ppermute | solution.py:18
  33.0 3.9 %collective-permute-start.9 = (f32[8,1,16,128]{3,0,2,1:T(8,128)S(1)}, f32[8,1,16,128]{3,0,2,1:T(8,128)S(1)}, u32[]{:S(2)}, u32[]{:S(2)}) collective-permute-start(f32[8,1,16,128]{3,0,2,1:T(8,128)S(1)} %get-tuple-element.15), channel_id=1, source_target_pairs={{0,8},{8,16},{16,24},{1,9},{9,17},{17,25},{2,10},{10,18},{18,26},{... | collective-permute-start | bytes 196616 | tf_op jit(solution)/shard_map/ppermute | solution.py:15
  36.9 10.6 %collective-permute-start.10 = (f32[8,66,1,128]{3,0,2,1:T(8,128)S(1)}, f32[8,66,1,128]{3,0,2,1:T(8,128)S(1)}, u32[]{:S(2)}, u32[]{:S(2)}) collective-permute-start(f32[8,66,1,128]{3,0,2,1:T(8,128)S(1)} %get-tuple-element.11), channel_id=1, source_target_pairs={{1,0},{2,1},{3,2},{4,3},{5,4},{6,5},{7,6},{9,8},{10,9},{11,10},{12... | collective-permute-start | bytes 811016 | tf_op jit(solution)/shard_map/ppermute | solution.py:18
  38.2 16.6 %collective-permute-start.11 = (f32[8,66,1,128]{3,0,2,1:T(8,128)S(1)}, f32[8,66,1,128]{3,0,2,1:T(8,128)S(1)}, u32[]{:S(2)}, u32[]{:S(2)}) collective-permute-start(f32[8,66,1,128]{3,0,2,1:T(8,128)S(1)} %get-tuple-element.12), channel_id=1, source_target_pairs={{0,1},{1,2},{2,3},{3,4},{4,5},{5,6},{6,7},{8,9},{9,10},{10,11},{11... | collective-permute-start | bytes 811016 | tf_op jit(solution)/shard_map/ppermute | solution.py:15
  63.1 11.2 %copy-start.3 = (f32[8,64,16,128]{3,0,2,1:T(8,128)}, f32[8,64,16,128]{3,0,2,1:T(8,128)S(1)}, u32[]{:S(2)}) copy-start(f32[8,64,16,128]{3,0,2,1:T(8,128)S(1)} %get-tuple-element.5) | copy-start | bytes 12582916
  74.3 34.3 %collective-permute-start.12 = (f32[8,1,16,128]{3,0,2,1:T(8,128)S(1)}, f32[8,1,16,128]{3,0,2,1:T(8,128)S(1)}, u32[]{:S(2)}, u32[]{:S(2)}) collective-permute-start(f32[8,1,16,128]{3,0,2,1:T(8,128)S(1)} %get-tuple-element.14), channel_id=1, source_target_pairs={{8,0},{16,8},{24,16},{9,1},{17,9},{25,17},{10,2},{18,10},{26,18},{... | collective-permute-start | bytes 196616 | tf_op jit(solution)/shard_map/ppermute | solution.py:18
  75.6 33.0 %collective-permute-start.13 = (f32[8,1,16,128]{3,0,2,1:T(8,128)S(1)}, f32[8,1,16,128]{3,0,2,1:T(8,128)S(1)}, u32[]{:S(2)}, u32[]{:S(2)}) collective-permute-start(f32[8,1,16,128]{3,0,2,1:T(8,128)S(1)} %get-tuple-element.13), channel_id=1, source_target_pairs={{0,8},{8,16},{16,24},{1,9},{9,17},{17,25},{2,10},{10,18},{18,26},{... | collective-permute-start | bytes 196616 | tf_op jit(solution)/shard_map/ppermute | solution.py:15
  108.6 15.1 %copy-start.4 = (f32[8,64,16,128]{3,0,2,1:T(8,128)S(1)}, f32[8,64,16,128]{3,0,2,1:T(8,128)}, u32[]{:S(2)}) copy-start(f32[8,64,16,128]{3,0,2,1:T(8,128)} %copy-done.3) | copy-start | bytes 12582916
  108.6 15.1 %copy-start.13 = (f32[64,16,128]{2,1,0:T(8,128)S(1)}, f32[64,16,128]{2,1,0:T(8,128)}, u32[]{:S(2)}) copy-start(f32[64,16,128]{2,1,0:T(8,128)} %param.9) | copy-start | bytes 1572868
  109.9 10.2 %collective-permute-start.14 = (f32[8,66,1,128]{3,0,2,1:T(8,128)S(1)}, f32[8,66,1,128]{3,0,2,1:T(8,128)S(1)}, u32[]{:S(2)}, u32[]{:S(2)}) collective-permute-start(f32[8,66,1,128]{3,0,2,1:T(8,128)S(1)} %get-tuple-element.9), channel_id=1, source_target_pairs={{1,0},{2,1},{3,2},{4,3},{5,4},{6,5},{7,6},{9,8},{10,9},{11,10},{12... | collective-permute-start | bytes 811016 | tf_op jit(solution)/shard_map/ppermute | solution.py:18
  111.5 12.2 %collective-permute-start.15 = (f32[8,66,1,128]{3,0,2,1:T(8,128)S(1)}, f32[8,66,1,128]{3,0,2,1:T(8,128)S(1)}, u32[]{:S(2)}, u32[]{:S(2)}) collective-permute-start(f32[8,66,1,128]{3,0,2,1:T(8,128)S(1)} %get-tuple-element.10), channel_id=1, source_target_pairs={{0,1},{1,2},{2,3},{3,4},{4,5},{5,6},{6,7},{8,9},{9,10},{10,11},{11... | collective-permute-start | bytes 811016 | tf_op jit(solution)/shard_map/ppermute | solution.py:15
  116.4 17.2 %copy-start.1 = (f32[8,64,16,128]{3,0,2,1:T(8,128)S(1)}, f32[8,64,16,128]{3,0,2,1:T(8,128)}, u32[]{:S(2)}) copy-start(f32[8,64,16,128]{3,0,2,1:T(8,128)} %copy-done) | copy-start | bytes 12582916
  116.4 17.2 %copy-start.6 = (f32[8,64,16,128]{3,0,2,1:T(8,128)S(1)}, f32[8,64,16,128]{3,0,2,1:T(8,128)}, u32[]{:S(2)}) copy-start(f32[8,64,16,128]{3,0,2,1:T(8,128)} %get-tuple-element.6) | copy-start | bytes 12582916
  131.6 2.0 copy-start.7
  188.1 7.5 %copy-start.2 = (f32[8,64,16,128]{3,0,2,1:T(8,128)S(1)}, f32[8,64,16,128]{3,0,2,1:T(8,128)}, u32[]{:S(2)}) copy-start(f32[8,64,16,128]{3,0,2,1:T(8,128)} %copy-done) | copy-start | bytes 12582916
  188.1 7.5 %copy-start.5 = (f32[8,64,16,128]{3,0,2,1:T(8,128)S(1)}, f32[8,64,16,128]{3,0,2,1:T(8,128)}, u32[]{:S(2)}) copy-start(f32[8,64,16,128]{3,0,2,1:T(8,128)} %copy-done.3) | copy-start | bytes 12582916
